TPU v7x, 32 devices: a whole 2x2x4 slice. The times are simulated.
32 devices in a mesh: groups: 2 (over x), chan: 16 (over z, y, core).
Axes of the slice: x: 2, y: 2, z: 4, core: 2. Of those that a mesh axis runs over, the one named last changes fastest.
Arguments:
- waveforms: bfloat16 [10240, 15360], P('chan', 'groups'), parts along dimension 1, may hold values from -250 to 250
- basis: bfloat16 [16, 10240, 200], P(None, 'chan'), may hold values from -1 to 1
- bounds: int32 [2, 768], replicated, may hold values from 0 to 5120, as said below
Outputs:
- detection: float32 [15360], P(('groups', 'chan')), parts along dimension 0
- coefficients: float32 [16, 15360], P(None, ('groups', 'chan')), parts along dimension 1
There are 2 independent parts, one for each index of `groups`. A program takes and returns all parts, laid end to end along the dimension named above; an argument that names none is the same for every part. Nothing has to cross between parts.
Inputs may be any that keep to these rules, and one draw needn't show every extreme that they name: bounds[0, 0] is 0 and every bounds[0, f] is below 160; bounds[1, f] grows roughly in proportion to f and is 5120 at the last bin; where bounds[0, f] exceeds bounds[1, f] nothing passes.
All inputs are finite; a program needn't handle non-finite values.
Results may differ from a plain program's by a relative error of at most 0.017.
Values may be sent and summed in bfloat16 or wider, within the bound.
A program may use at most 128 MiB of HBM per device.

v0:
```python
import math
import jax
import jax.numpy as jnp
from jax import lax
from jax.sharding import PartitionSpec as P

time_blocks = 4
basis_blocks = 4
highest = lax.Precision.HIGHEST


def angle_lookup(row_ids, col_ids, modulus):
    rotation_radians = (row_ids[:, None] * col_ids[None, :] % modulus).astype(jnp.float32) * (
        2.0 * math.pi / modulus
    )
    return (jnp.cos(rotation_radians), jnp.sin(rotation_radians))


def rotate(layout, cos_table, sin_table, real_part, imag_part, orientation):
    cos_real = jnp.einsum(layout, cos_table, real_part, precision=highest)
    cos_imag = jnp.einsum(layout, cos_table, imag_part, precision=highest)
    sin_real = jnp.einsum(layout, sin_table, real_part, precision=highest)
    sin_imag = jnp.einsum(layout, sin_table, imag_part, precision=highest)
    return (cos_real - orientation * sin_imag, cos_imag + orientation * sin_real)


def apply_twist(cos_table, sin_table, real_part, imag_part, orientation):
    return (
        cos_table * real_part - orientation * sin_table * imag_part,
        cos_table * imag_part + orientation * sin_table * real_part,
    )


def count_ids(count):
    return jnp.arange(count, dtype=jnp.int32)


def block_table(base_tables, freq_ids, offset, recorded_readings):
    base_cos, base_sin = base_tables
    shift_cos, shift_sin = angle_lookup(freq_ids, jnp.reshape(offset, (1,)), recorded_readings)
    cos_table = base_cos * shift_cos - base_sin * shift_sin
    sin_table = base_sin * shift_cos + base_cos * shift_sin
    return jnp.stack([cos_table, -sin_table]).astype(jnp.bfloat16)


def temporal_spectrum(waveforms, base_tables, layout, output_dims):
    recorded_readings = waveforms.shape[1]
    block_width = recorded_readings // time_blocks
    freq_ids = count_ids(base_tables[0].shape[0])

    def temporal_advance(running, block_id):
        offset = block_id * block_width
        dft_table = block_table(base_tables, freq_ids, offset, recorded_readings)
        segment = lax.dynamic_slice_in_dim(waveforms, offset, block_width, 1)
        return (
            running + jnp.einsum(layout, dft_table, segment, preferred_element_type=jnp.float32),
            None,
        )

    spectrum, _ = lax.scan(
        temporal_advance, jnp.zeros(output_dims, jnp.float32), count_ids(time_blocks)
    )
    return spectrum.astype(jnp.bfloat16)


def frequency_filter(local_spectrum, band_edges):
    values = local_spectrum.astype(jnp.float32)
    bin_count, full_count = (values.shape[1], values.shape[2])
    devices = lax.axis_size("chan")
    block_width = full_count // devices
    real_part = values[0].reshape(bin_count, devices, block_width)
    imag_part = values[1].reshape(bin_count, devices, block_width)
    cos_parts, sine_components = angle_lookup(count_ids(devices), count_ids(devices), devices)
    cos_width, sin_width = angle_lookup(count_ids(block_width), count_ids(block_width), block_width)
    cos_twist, sin_twist = angle_lookup(count_ids(devices), count_ids(block_width), full_count)
    real_part, imag_part = rotate(
        "kp,fpm->fkm", cos_parts, sine_components, real_part, imag_part, -1.0
    )
    real_part, imag_part = apply_twist(cos_twist, sin_twist, real_part, imag_part, -1.0)
    real_part, imag_part = rotate("mn,fkm->fkn", cos_width, sin_width, real_part, imag_part, -1.0)
    wave_ids = count_ids(devices)[:, None] + devices * count_ids(block_width)[None, :]
    magnitude = jnp.where(wave_ids > full_count // 2, full_count - wave_ids, wave_ids)[None]
    passing = (magnitude >= band_edges[0][:, None, None]) & (
        magnitude <= band_edges[1][:, None, None]
    )
    real_part = jnp.where(passing, real_part, 0.0)
    imag_part = jnp.where(passing, imag_part, 0.0)
    real_part, imag_part = rotate("mn,fkn->fkm", cos_width, sin_width, real_part, imag_part, 1.0)
    real_part, imag_part = apply_twist(cos_twist, sin_twist, real_part, imag_part, 1.0)
    real_part, imag_part = rotate(
        "kp,fkm->fpm", cos_parts, sine_components, real_part, imag_part, 1.0
    )
    restored = jnp.stack([real_part, imag_part]).reshape(2, bin_count, full_count) * (
        1.0 / full_count
    )
    return restored.astype(jnp.bfloat16)


def coefficient_spectra(basis, filtered, layout, frequencies, recorded_readings):
    basis_rank, channels, tap_count = basis.shape
    cos_table, sin_table = angle_lookup(
        count_ids(frequencies), count_ids(tap_count), recorded_readings
    )
    dft_table = jnp.stack([cos_table, -sin_table]).astype(jnp.bfloat16)
    filtered_real = filtered[0].astype(jnp.float32)
    filtered_imag = filtered[1].astype(jnp.float32)
    contract = "kfm," + layout + "->kf"
    basis_group = basis.reshape(basis_blocks, basis_rank // basis_blocks, channels, tap_count)

    def project(members):
        transformed = jnp.einsum(
            "kml,rfl->krfm", members, dft_table, preferred_element_type=jnp.float32
        )
        trans_real, trans_imag = (transformed[:, 0], transformed[:, 1])
        spectra_real = jnp.einsum(
            contract, trans_real, filtered_real, precision=highest
        ) + jnp.einsum(contract, trans_imag, filtered_imag, precision=highest)
        fourier_quadrature = jnp.einsum(
            contract, trans_real, filtered_imag, precision=highest
        ) - jnp.einsum(contract, trans_imag, filtered_real, precision=highest)
        return jnp.stack([spectra_real, fourier_quadrature], axis=1)

    return lax.map(project, basis_group).reshape(basis_rank, 2, frequencies)


def channel_power(filtered, base_tables, layout, frequencies, recorded_readings):
    freq_ids = count_ids(frequencies)
    weights = jnp.where(freq_ids == 0, 1.0, 2.0).astype(jnp.bfloat16)
    weighted = filtered * weights[None, :, None]
    block_width = recorded_readings // time_blocks
    contract = "r" + layout + ",rft->mt"

    def channel_advance(running, block_id):
        offset = block_id * block_width
        dft_table = block_table(base_tables, freq_ids, offset, recorded_readings)
        traces = jnp.einsum(contract, weighted, dft_table, preferred_element_type=jnp.float32) * (
            1.0 / recorded_readings
        )
        return (running, jnp.sum(traces * traces, axis=0))

    _, pieces = lax.scan(channel_advance, jnp.zeros((), jnp.float32), count_ids(time_blocks))
    return pieces.reshape(recorded_readings)


def local(waveforms, basis, bounds):
    devices = lax.axis_size("chan")
    position = lax.axis_index("chan")
    channels, recorded_readings = waveforms.shape
    basis_rank, _, tap_count = basis.shape
    frequencies = bounds.shape[1]
    full_count = channels * devices
    freq_ids = count_ids(frequencies)
    base_tables = angle_lookup(
        freq_ids, count_ids(recorded_readings // time_blocks), recorded_readings
    )
    layout = "fm"
    spectrum = temporal_spectrum(waveforms, base_tables, "rft,mt->rfm", (2, frequencies, channels))
    local_spectrum = lax.all_to_all(spectrum, "chan", split_axis=1, concat_axis=2, tiled=True)
    bin_count = local_spectrum.shape[1]
    band_edges = lax.dynamic_slice_in_dim(bounds, position * bin_count, bin_count, 1)
    filtered = lax.all_to_all(
        frequency_filter(local_spectrum, band_edges),
        "chan",
        split_axis=2,
        concat_axis=1,
        tiled=True,
    )
    spectra = coefficient_spectra(basis, filtered, layout, frequencies, recorded_readings)
    flattened = basis.reshape(basis_rank, channels * tap_count)
    gram_matrix = jnp.einsum("ka,ja->kj", flattened, flattened, preferred_element_type=jnp.float32)
    trace_power = channel_power(filtered, base_tables, layout, frequencies, recorded_readings)
    spectra, gram_matrix, trace_power = lax.psum((spectra, gram_matrix, trace_power), "chan")
    lag_count = recorded_readings // devices
    lag_start = position * lag_count
    cos_lags, sin_lags = angle_lookup(freq_ids, lag_start + count_ids(lag_count), recorded_readings)
    weights = jnp.where(freq_ids == 0, 1.0, 2.0).astype(jnp.float32)
    scaled_inphase = spectra[:, 0] * weights[None, :]
    weighted_imag = spectra[:, 1] * weights[None, :]
    correlation = (
        jnp.dot(scaled_inphase, cos_lags, precision=highest)
        - jnp.dot(weighted_imag, sin_lags, precision=highest)
    ) * (1.0 / recorded_readings)
    extended = jnp.concatenate([trace_power, trace_power[:tap_count]])
    running = jnp.concatenate([jnp.zeros((1,), jnp.float32), jnp.cumsum(extended)])
    energy = lax.dynamic_slice_in_dim(
        running, lag_start + tap_count, lag_count, 0
    ) - lax.dynamic_slice_in_dim(running, lag_start, lag_count, 0)
    energy_threshold = energy / (full_count * tap_count) + 1e-06
    cholesky_factor = jnp.linalg.cholesky(gram_matrix)
    solved = jax.scipy.linalg.cho_solve((cholesky_factor, True), correlation)
    detection = jnp.sum(correlation * solved, axis=0) / (basis_rank * energy_threshold)
    coefficients = correlation / jnp.sqrt(energy_threshold)[None, :]
    return (detection, coefficients)


def solution(mesh):
    in_specs = (P("chan", "groups"), P(None, "chan", None), P())
    out_specs = (P(("groups", "chan")), P(None, ("groups", "chan")))
    return jax.shard_map(local, mesh=mesh, in_specs=in_specs, out_specs=out_specs, check_vma=False)
```

profile of v0, /device:TPU:0, one launch (start us, length us, event | category | flops | bytes accessed | tf_op | source)
XLA Modules:
  0.0 827.4 jit_solution(9234787007890897605)
XLA Ops:
  7.2 148.7 %while.40 = (s32[]{:T(128)}, f32[2,768,640]{2,1,0:T(8,128)}, s32[4]{0:T(128)S(1)}, bf16[640,7680]{1,0:T(8,128)(2,1)}, s32[]{:T(128)}, /*index=5*/s32[]{:T(128)}, s32[1]{0:T(128)}, s32[]{:T(128)}) while((s32[]{:T(128)}, f32[2,768,640]{2,1,0:T(8,128)}, s32[4]{0:T(128)S(1)}, bf16[640,7680]{1,0:T(8,128)(2,1)}, s32[]{:T(128)}, ...), condition=%wide.region_1.2_spmd.clone.clone, body=%wide.region_0.1_spmd.clone.clone.sunk | while | flops 3806337792 | bytes 53588192 | solution.py:60
  8.5 25.9 %fusion.331 = (bf16[1,768,1920]{2,1,0:T(8,128)(2,1)S(1)}, bf16[1,768,1920]{2,1,0:T(8,128)(2,1)S(1)}) fusion(f32[768]{0:T(1024)S(1)} %get-tuple-element.499, f32[768]{0:T(1024)S(1)} %get-tuple-element.500), kind=kLoop, calls=%fused_computation.52.clone.1 | loop fusion | flops 26542080 | bytes 5904384 | tf_op jit(solution)/shard_map/convert
  34.5 8.1 select_add_fusion.2
  45.7 25.9 %fusion.331 = (bf16[1,768,1920]{2,1,0:T(8,128)(2,1)S(1)}, bf16[1,768,1920]{2,1,0:T(8,128)(2,1)S(1)}) fusion(f32[768]{0:T(1024)S(1)} %get-tuple-element.499, f32[768]{0:T(1024)S(1)} %get-tuple-element.500), kind=kLoop, calls=%fused_computation.52.clone.1 | loop fusion | flops 26542080 | bytes 5904384 | tf_op jit(solution)/shard_map/convert
  71.6 8.0 select_add_fusion.2
  82.9 25.9 %fusion.331 = (bf16[1,768,1920]{2,1,0:T(8,128)(2,1)S(1)}, bf16[1,768,1920]{2,1,0:T(8,128)(2,1)S(1)}) fusion(f32[768]{0:T(1024)S(1)} %get-tuple-element.499, f32[768]{0:T(1024)S(1)} %get-tuple-element.500), kind=kLoop, calls=%fused_computation.52.clone.1 | loop fusion | flops 26542080 | bytes 5904384 | tf_op jit(solution)/shard_map/convert
  108.8 8.1 select_add_fusion.2
  120.1 25.9 %fusion.331 = (bf16[1,768,1920]{2,1,0:T(8,128)(2,1)S(1)}, bf16[1,768,1920]{2,1,0:T(8,128)(2,1)S(1)}) fusion(f32[768]{0:T(1024)S(1)} %get-tuple-element.499, f32[768]{0:T(1024)S(1)} %get-tuple-element.500), kind=kLoop, calls=%fused_computation.52.clone.1 | loop fusion | flops 26542080 | bytes 5904384 | tf_op jit(solution)/shard_map/convert
  146.0 8.0 select_add_fusion.2
  155.9 6.4 copy.169
  162.4 7.6 all-to-all-start
  170.5 38.0 %all-to-all-done = bf16[2,768,640]{2,0,1:T(2,128)(2,1)S(1)} async-done(((bf16[2,768,640]{2,0,1:T(2,128)(2,1)}), bf16[2,768,640]{2,0,1:T(2,128)(2,1)S(1)}, u32[]{:S(2)}, u32[]{:S(2)}) %all-to-all-start) | async-done | bytes 1966112 | tf_op jit(solution)/shard_map/all_to_all | solution.py:158
  213.6 11.9 %fusion.89 = f32[48,16,640]{2,1,0:T(8,128)S(1)} fusion(f32[48,640,16]{1,2,0:T(8,128)S(1)} %multiply_add_fusion.1, f32[48,640,16]{1,2,0:T(8,128)S(1)} %multiply_subtract_fusion.1, f32[16,640]{1,0:T(8,128)S(1)} %get-tuple-element.385, f32[16,640]{1,0:T(8,128)S(1)} %get-tuple-element.384), kind=kOutput, calls=%fused_computation.124 | convolution fusion | flops 3780034560 | bytes 5980160 | tf_op jit(solution)/shard_map/mn,fkm->fkn/dot_general | solution.py:22
  225.5 11.7 %fusion.91 = f32[48,16,640]{2,1,0:T(8,128)S(1)} fusion(f32[48,640,16]{1,2,0:T(8,128)S(1)} %multiply_add_fusion.1, f32[48,640,16]{1,2,0:T(8,128)S(1)} %multiply_subtract_fusion.1, f32[16,640]{1,0:T(8,128)S(1)} %get-tuple-element.385, f32[16,640]{1,0:T(8,128)S(1)} %get-tuple-element.384), kind=kOutput, calls=%fused_computation.126 | convolution fusion | flops 3780034560 | bytes 5980160 | tf_op jit(solution)/shard_map/mn,fkm->fkn/dot_general | solution.py:23
  237.3 11.8 %add_select_fusion.6 = f32[48,16,640]{2,1,0:T(8,128)S(1)} fusion(f32[48,16,640]{2,1,0:T(8,128)S(1)} %fusion.89, s32[16,640]{1,0:T(8,128)S(1)} %compare_select_fusion, s32[48]{0:T(128)S(1)} %get-tuple-element.381, s32[48]{0:T(128)S(1)} %get-tuple-element.380, f32[48,640,16]{1,2,0:T(8,128)S(1)} %multiply_add_fusion.1, ...), kind=kOutput, calls=%fused_computation.113 | convolution fusion | flops 3782983680 | bytes 7987584 | tf_op jit(solution)/shard_map/mn,fkm->fkn/dot_general | solution.py:21
  249.0 11.8 %fusion.87 = f32[48,16,640]{2,1,0:T(8,128)S(1)} fusion(f32[48,16,640]{2,1,0:T(8,128)S(1)} %add_select_fusion.6), kind=kOutput, calls=%fused_computation.122 | convolution fusion | flops 3778560000 | bytes 3932160 | tf_op jit(solution)/shard_map/mn,fkn->fkm/dot_general | solution.py:23
  260.9 11.7 %subtract_select_fusion = f32[48,16,640]{2,1,0:T(8,128)S(1)} fusion(f32[48,16,640]{2,1,0:T(8,128)S(1)} %fusion.91, s32[16,640]{1,0:T(8,128)S(1)} %compare_select_fusion, s32[48]{0:T(128)S(1)} %get-tuple-element.381, s32[48]{0:T(128)S(1)} %get-tuple-element.380, f32[48,640,16]{1,2,0:T(8,128)S(1)} %multiply_add_fusion.1, ...), kind=kOutput, calls=%fused_computation.114 | convolution fusion | flops 3782983680 | bytes 7987584 | tf_op jit(solution)/shard_map/mn,fkm->fkn/dot_general | solution.py:20
  272.6 11.6 %fusion.85 = f32[48,16,640]{2,1,0:T(8,128)S(1)} fusion(f32[48,16,640]{2,1,0:T(8,128)S(1)} %subtract_select_fusion), kind=kOutput, calls=%fused_computation.120 | convolution fusion | flops 3778560000 | bytes 3932160 | tf_op jit(solution)/shard_map/mn,fkn->fkm/dot_general | solution.py:22
  284.2 11.9 %fusion.114 = f32[48,16,640]{2,1,0:T(8,128)S(1)} fusion(f32[48,16,640]{2,1,0:T(8,128)S(1)} %fusion.87, f32[48,16,640]{2,1,0:T(8,128)S(1)} %subtract_select_fusion), kind=kOutput, calls=%fused_computation.142 | convolution fusion | flops 3779051520 | bytes 5898240 | tf_op jit(solution)/shard_map/mn,fkn->fkm/dot_general | solution.py:20
  296.2 11.5 %fusion.117 = f32[48,16,640]{2,1,0:T(8,128)S(1)} fusion(f32[48,16,640]{2,1,0:T(8,128)S(1)} %fusion.85, f32[48,16,640]{2,1,0:T(8,128)S(1)} %add_select_fusion.6), kind=kOutput, calls=%fused_computation.143 | convolution fusion | flops 3779051520 | bytes 5898240 | tf_op jit(solution)/shard_map/mn,fkn->fkm/dot_general | solution.py:21
  307.7 2.0 fusion.185
  309.8 3.3 fusion.184
  313.1 3.3 add_bitcast_fusion.1
  316.4 2.8 stack.44
  319.2 5.5 subtract_bitcast_fusion.1
  324.7 2.9 stack.43
  327.6 3.4 fusion.80
  331.0 11.3 %copy.99 = bf16[2,48,10240]{1,0,2:T(2,128)(2,1)} copy(bf16[2,48,10240]{2,1,0:T(8,128)(2,1)} %fusion.80) | data formatting | bytes 3932160 | tf_op jit(solution)/shard_map/convert_element_type | solution.py:96
  342.2 10.5 %reshape.584 = bf16[16,2,30720]{2,1,0:T(2,128)(2,1)} reshape(bf16[10240,2,48]{2,1,0:T(2,128)(2,1)} %bitcast.263) | data formatting | bytes 3932160
  352.7 10.7 %all-to-all-start.1 = ((bf16[16,2,30720]{2,1,0:T(2,128)(2,1)}), bf16[16,2,30720]{2,1,0:T(2,128)(2,1)S(1)}, u32[]{:S(2)}, u32[]{:S(2)}) async-start(bf16[16,2,30720]{2,1,0:T(2,128)(2,1)} %reshape.584), calls=%async_computation.1 | async-start | bytes 3932160 | tf_op jit(solution)/shard_map/all_to_all | solution.py:161
  363.5 2.6 negate_convert_fusion
  366.2 5.1 fusion.142
  371.3 30.8 %all-to-all-done.1 = bf16[16,2,30720]{2,1,0:T(2,128)(2,1)S(1)} async-done(((bf16[16,2,30720]{2,1,0:T(2,128)(2,1)}), bf16[16,2,30720]{2,1,0:T(2,128)(2,1)S(1)}, u32[]{:S(2)}, u32[]{:S(2)}) %all-to-all-start.1) | async-done | bytes 1966112 | tf_op jit(solution)/shard_map/all_to_all | solution.py:161
  402.1 6.7 reshape.585
  408.8 9.6 %copy.148 = bf16[2,48,16,640]{3,1,2,0:T(8,128)(2,1)S(1)} copy(bf16[2,48,16,640]{1,0,3,2:T(2,128)(2,1)} %bitcast.261) | data formatting | bytes 3932160 | tf_op jit(solution)/shard_map/all_to_all | solution.py:161
  418.4 8.8 %copy.146 = bf16[2,48,16,640]{3,2,1,0:T(8,128)(2,1)} copy(bf16[2,48,16,640]{1,0,3,2:T(2,128)(2,1)} %bitcast.262) | data formatting | bytes 3932160 | tf_op jit(solution)/shard_map/all_to_all | solution.py:161
  428.9 4.1 copy.109
  433.0 126.7 %while.39 = (s32[]{:T(128)}, f32[4,1920]{1,0:T(4,128)S(1)}, s32[4]{0:T(128)S(1)}, bf16[2,768,640]{1,2,0:T(8,128)(2,1)}, s32[]{:T(128)}, /*index=5*/s32[1]{0:T(128)}, s32[]{:T(128)}) while((s32[]{:T(128)}, f32[4,1920]{1,0:T(4,128)S(1)}, s32[4]{0:T(128)S(1)}, bf16[2,768,640]{1,2,0:T(8,128)(2,1)}, s32[]{:T(128)}, ...), condition=%wide.region_11.12_spmd.clone.clone, body=%wide.region_9.11_spmd.clone.clone.sunk | while | flops 3808056064 | bytes 21677712 | solution.py:141
  434.3 25.9 %fusion.326 = (bf16[1,768,1920]{2,1,0:T(8,128)(2,1)S(1)}, bf16[1,768,1920]{2,1,0:T(8,128)(2,1)S(1)}) fusion(f32[768]{0:T(1024)S(1)} %get-tuple-element.491, f32[768]{0:T(1024)S(1)} %get-tuple-element.492), kind=kLoop, calls=%fused_computation.16.clone.1 | loop fusion | flops 26542080 | bytes 5904384 | tf_op jit(solution)/shard_map/convert.2
  460.3 4.3 fusion.327
  466.0 25.9 %fusion.326 = (bf16[1,768,1920]{2,1,0:T(8,128)(2,1)S(1)}, bf16[1,768,1920]{2,1,0:T(8,128)(2,1)S(1)}) fusion(f32[768]{0:T(1024)S(1)} %get-tuple-element.491, f32[768]{0:T(1024)S(1)} %get-tuple-element.492), kind=kLoop, calls=%fused_computation.16.clone.1 | loop fusion | flops 26542080 | bytes 5904384 | tf_op jit(solution)/shard_map/convert.2
  491.9 4.3 fusion.327
  497.7 25.9 %fusion.326 = (bf16[1,768,1920]{2,1,0:T(8,128)(2,1)S(1)}, bf16[1,768,1920]{2,1,0:T(8,128)(2,1)S(1)}) fusion(f32[768]{0:T(1024)S(1)} %get-tuple-element.491, f32[768]{0:T(1024)S(1)} %get-tuple-element.492), kind=kLoop, calls=%fused_computation.16.clone.1 | loop fusion | flops 26542080 | bytes 5904384 | tf_op jit(solution)/shard_map/convert.2
  523.6 4.3 fusion.327
  529.3 25.9 %fusion.326 = (bf16[1,768,1920]{2,1,0:T(8,128)(2,1)S(1)}, bf16[1,768,1920]{2,1,0:T(8,128)(2,1)S(1)}) fusion(f32[768]{0:T(1024)S(1)} %get-tuple-element.491, f32[768]{0:T(1024)S(1)} %get-tuple-element.492), kind=kLoop, calls=%fused_computation.16.clone.1 | loop fusion | flops 26542080 | bytes 5904384 | tf_op jit(solution)/shard_map/convert.2
  555.3 4.3 fusion.327
  559.7 67.2 %all-reduce.1 = (f32[16,16]{0,1:T(8,128)S(1)}, f32[7680]{0:T(1024)S(1)}) all-reduce(f32[16,16]{0,1:T(8,128)S(1)} %fusion.142, f32[7680]{0:T(1024)S(1)} %reshape.545), channel_id=1, replica_groups=mesh['groups'=2,'chan'=16] {'chan'}, use_global_device_ids=true, to_apply=%region_5.6 | all-reduce | flops 7936 | bytes 63488 | tf_op jit(solution)/shard_map/psum | solution.py:172
  629.8 1.9 copy.102
  631.7 84.8 %while.38 = (s32[]{:T(128)}, f32[4,4,2,768]{3,2,1,0:T(2,128)S(1)}, bf16[4,4,640,200]{2,3,1,0:T(8,128)(2,1)}, bf16[2,768,200]{1,2,0:T(8,128)(2,1)S(1)}, f32[768,640]{1,0:T(8,128)}, /*index=5*/f32[768,640]{1,0:T(8,128)}, s32[]{:T(128)}) while((s32[]{:T(128)}, f32[4,4,2,768]{3,2,1,0:T(2,128)S(1)}, bf16[4,4,640,200]{2,3,1,0:T(8,128)(2,1)}, ...), condition=%wide.region_3.4_spmd, body=%wide.region_2.3_spmd.sunk | while | flops 1588592640 | bytes 45113436 | solution.py:123
  631.7 9.1 %convolution_bitcast_fusion.2 = f32[4,2,768,640]{2,3,1,0:T(8,128)} fusion(bf16[4,4,640,200]{2,3,1,0:T(8,128)(2,1)} %get-tuple-element.564, s32[]{:T(128)S(6)} %copy.193, bf16[2,768,200]{1,2,0:T(8,128)(2,1)S(1)} %get-tuple-element.565), kind=kOutput, calls=%fused_computation.79.clone.1 | convolution fusion | flops 1572864000 | bytes 17367044 | tf_op jit(solution)/shard_map/while/body/eval_jaxpr/kml,rfl->krfm/dot_general | solution.py:111
  642.6 2.9 copy.176
  645.6 7.2 multiply_reduce_fusion.5
  652.9 9.1 %convolution_bitcast_fusion.2 = f32[4,2,768,640]{2,3,1,0:T(8,128)} fusion(bf16[4,4,640,200]{2,3,1,0:T(8,128)(2,1)} %get-tuple-element.564, s32[]{:T(128)S(6)} %copy.193, bf16[2,768,200]{1,2,0:T(8,128)(2,1)S(1)} %get-tuple-element.565), kind=kOutput, calls=%fused_computation.79.clone.1 | convolution fusion | flops 1572864000 | bytes 17367044 | tf_op jit(solution)/shard_map/while/body/eval_jaxpr/kml,rfl->krfm/dot_general | solution.py:111
  663.8 2.9 copy.176
  666.8 7.2 multiply_reduce_fusion.5
  674.1 9.1 %convolution_bitcast_fusion.2 = f32[4,2,768,640]{2,3,1,0:T(8,128)} fusion(bf16[4,4,640,200]{2,3,1,0:T(8,128)(2,1)} %get-tuple-element.564, s32[]{:T(128)S(6)} %copy.193, bf16[2,768,200]{1,2,0:T(8,128)(2,1)S(1)} %get-tuple-element.565), kind=kOutput, calls=%fused_computation.79.clone.1 | convolution fusion | flops 1572864000 | bytes 17367044 | tf_op jit(solution)/shard_map/while/body/eval_jaxpr/kml,rfl->krfm/dot_general | solution.py:111
  685.0 2.9 copy.176
  688.0 7.2 multiply_reduce_fusion.5
  695.3 9.1 %convolution_bitcast_fusion.2 = f32[4,2,768,640]{2,3,1,0:T(8,128)} fusion(bf16[4,4,640,200]{2,3,1,0:T(8,128)(2,1)} %get-tuple-element.564, s32[]{:T(128)S(6)} %copy.193, bf16[2,768,200]{1,2,0:T(8,128)(2,1)S(1)} %get-tuple-element.565), kind=kOutput, calls=%fused_computation.79.clone.1 | convolution fusion | flops 1572864000 | bytes 17367044 | tf_op jit(solution)/shard_map/while/body/eval_jaxpr/kml,rfl->krfm/dot_general | solution.py:111
  706.2 2.9 copy.176
  709.2 7.2 multiply_reduce_fusion.5
  721.3 82.0 %all-reduce.4.cloned.1.call-done = f32[16,2,768]{2,1,0:T(2,128)} async-done(((f32[16,2,768]{2,1,0:T(2,128)}), f32[16,2,768]{2,1,0:T(2,128)}) %all-reduce.4.cloned.1.call-update) | async-done | bytes 98320 | tf_op jit(solution)/shard_map/psum | solution.py:172
  804.4 6.9 fusion.122
  811.3 7.7 broadcast_divide_fusion
  (125 shorter events, 38.3 us)
Async XLA Ops:
  7.2 162.8 %copy-start = (s32[2,768]{1,0:T(2,128)S(1)}, s32[2,768]{1,0:T(2,128)}, u32[]{:S(2)}) copy-start(s32[2,768]{1,0:T(2,128)} %param.11) | copy-start | bytes 18436
  8.5 25.9 %copy-start.5 = (f32[2,768,640]{2,1,0:T(8,128)S(1)}, f32[2,768,640]{2,1,0:T(8,128)}, u32[]{:S(2)}) copy-start(f32[2,768,640]{2,1,0:T(8,128)} %get-tuple-element.512) | copy-start | bytes 11796484 | tf_op jit(solution)/shard_map/while
  42.5 1.9 copy-start.6
  45.7 25.9 %copy-start.5 = (f32[2,768,640]{2,1,0:T(8,128)S(1)}, f32[2,768,640]{2,1,0:T(8,128)}, u32[]{:S(2)}) copy-start(f32[2,768,640]{2,1,0:T(8,128)} %get-tuple-element.512) | copy-start | bytes 11796484 | tf_op jit(solution)/shard_map/while
  79.7 1.9 copy-start.6
  82.9 25.9 %copy-start.5 = (f32[2,768,640]{2,1,0:T(8,128)S(1)}, f32[2,768,640]{2,1,0:T(8,128)}, u32[]{:S(2)}) copy-start(f32[2,768,640]{2,1,0:T(8,128)} %get-tuple-element.512) | copy-start | bytes 11796484 | tf_op jit(solution)/shard_map/while
  116.9 1.9 copy-start.6
  120.1 25.9 %copy-start.5 = (f32[2,768,640]{2,1,0:T(8,128)S(1)}, f32[2,768,640]{2,1,0:T(8,128)}, u32[]{:S(2)}) copy-start(f32[2,768,640]{2,1,0:T(8,128)} %get-tuple-element.512) | copy-start | bytes 11796484 | tf_op jit(solution)/shard_map/while
  154.1 1.9 copy-start.6
  162.4 46.1 %all-to-all-start = ((bf16[2,768,640]{2,0,1:T(2,128)(2,1)}), bf16[2,768,640]{2,0,1:T(2,128)(2,1)S(1)}, u32[]{:S(2)}, u32[]{:S(2)}) async-start(bf16[2,768,640]{2,0,1:T(2,128)(2,1)} %copy.169), calls=%async_computation | async-start | bytes 3932160 | tf_op jit(solution)/shard_map/all_to_all | solution.py:158
  307.7 5.4 copy-start.2
  324.7 2.9 copy-start.4
  352.7 49.4 %all-to-all-start.1 = ((bf16[16,2,30720]{2,1,0:T(2,128)(2,1)}), bf16[16,2,30720]{2,1,0:T(2,128)(2,1)S(1)}, u32[]{:S(2)}, u32[]{:S(2)}) async-start(bf16[16,2,30720]{2,1,0:T(2,128)(2,1)} %reshape.584), calls=%async_computation.1 | async-start | bytes 3932160 | tf_op jit(solution)/shard_map/all_to_all | solution.py:161
  363.4 439.9 %all-reduce.4.cloned.1.call-start = ((), (), s32[]{:S(2)}) async-start(), calls=%async_computation.2 | async-start | bytes 196608 | tf_op jit(solution)/shard_map/psum | solution.py:172
  433.0 194.6 %copy-start.3 = (bf16[2,48,16,640]{3,2,1,0:T(8,128)(2,1)S(1)}, bf16[2,48,16,640]{3,2,1,0:T(8,128)(2,1)}, u32[]{:S(2)}) copy-start(bf16[2,48,16,640]{3,2,1,0:T(8,128)(2,1)} %copy.146) | copy-start | bytes 5898244
  434.3 25.9 %copy-start.7 = (bf16[2,768,640]{1,2,0:T(8,128)(2,1)S(1)}, bf16[2,768,640]{1,2,0:T(8,128)(2,1)}, u32[]{:S(2)}) copy-start(bf16[2,768,640]{1,2,0:T(8,128)(2,1)} %get-tuple-element.544) | copy-start | bytes 5898244 | tf_op jit(solution)/shard_map/while
  466.0 25.9 %copy-start.7 = (bf16[2,768,640]{1,2,0:T(8,128)(2,1)S(1)}, bf16[2,768,640]{1,2,0:T(8,128)(2,1)}, u32[]{:S(2)}) copy-start(bf16[2,768,640]{1,2,0:T(8,128)(2,1)} %get-tuple-element.544) | copy-start | bytes 5898244 | tf_op jit(solution)/shard_map/while
  497.7 25.9 %copy-start.7 = (bf16[2,768,640]{1,2,0:T(8,128)(2,1)S(1)}, bf16[2,768,640]{1,2,0:T(8,128)(2,1)}, u32[]{:S(2)}) copy-start(bf16[2,768,640]{1,2,0:T(8,128)(2,1)} %get-tuple-element.544) | copy-start | bytes 5898244 | tf_op jit(solution)/shard_map/while
  529.3 25.9 %copy-start.7 = (bf16[2,768,640]{1,2,0:T(8,128)(2,1)S(1)}, bf16[2,768,640]{1,2,0:T(8,128)(2,1)}, u32[]{:S(2)}) copy-start(bf16[2,768,640]{1,2,0:T(8,128)(2,1)} %get-tuple-element.544) | copy-start | bytes 5898244 | tf_op jit(solution)/shard_map/while
  716.5 0.6 copy-start.8
  811.3 8.7 %copy-start.1 = (s32[2,768]{1,0:T(2,128)S(1)}, s32[2,768]{1,0:T(2,128)}, u32[]{:S(2)}) copy-start(s32[2,768]{1,0:T(2,128)} %param.11) | copy-start | bytes 18436
Sparse Core Ops, SparseCore 0:
  717.3 86.0 all-reduce.3
where the time goes:
time: 837 us; the launch traced here: 827 us
  other arithmetic  250 us (30%)
  matrix products  218 us (26%)
  waiting for transfers between devices  151 us (18%)
  local copies, waits for them, and re-layouts  102 us (12%)
  blocking collectives  67.2 us (8%)
  starting transfers between devices  18.4 us (2%)
  between operations  14.9 us (2%)
    another operation x13, other arithmetic  210 us
    psum x1, waiting for transfers between devices, local(): lax.psum((spectra, gram_matrix, trace_power), 'chan')  82 us
    psum x1, blocking collectives, local(): lax.psum((spectra, gram_matrix, trace_power), 'chan')  67.2 us
    all_to_all x1, waiting for transfers between devices, local(): lax.all_to_all(spectrum, 'chan', split_axis=1, concat_axis=2, tiled=True)  38 us
    dot_general x4, matrix products, project(): jnp.einsum('kml,rfl->krfm', members, dft_table, preferred_element_type=jn...  36.2 us
    dot_general x4, matrix products, temporal_advance(): jnp.einsum(layout, dft_table, segment, preferred_element_type=jnp.float32)  32.2 us
    all_to_all x1, waiting for transfers between devices, local(): lax.all_to_all(frequency_filter(local_spectrum, band_edges), 'chan', spli...  30.8 us
    dot_general x4, matrix products, rotate(): sin_imag = jnp.einsum(layout, sin_table, imag_part, precision=highest)  30.2 us
  transfers between devices with their start and end apart: 3, of which 3 were waited for; matrix products, arithmetic and copies ran while one was open for 2% of the time, Pallas kernels for 0%

commit v1 on v0

--- a/solution.py
+++ b/solution.py
@@ -158,12 +158,18 @@
     local_spectrum = lax.all_to_all(spectrum, "chan", split_axis=1, concat_axis=2, tiled=True)
     bin_count = local_spectrum.shape[1]
     band_edges = lax.dynamic_slice_in_dim(bounds, position * bin_count, bin_count, 1)
-    filtered = lax.all_to_all(
-        frequency_filter(local_spectrum, band_edges),
-        "chan",
-        split_axis=2,
-        concat_axis=1,
-        tiled=True,
+    filtered = jnp.concatenate(
+        lax.all_to_all(
+            jnp.stack(
+                jnp.split(
+                    frequency_filter(local_spectrum, band_edges), lax.axis_size("chan"), axis=2
+                )
+            ),
+            "chan",
+            0,
+            0,
+        ),
+        axis=1,
     )
     spectra = coefficient_spectra(basis, filtered, layout, frequencies, recorded_readings)
     flattened = basis.reshape(basis_rank, channels * tap_count)

time: 837 us -> 800 us (0.956)
  local copies, waits for them, and re-layouts: 102 us -> 63.6 us
    all_to_all x2 -> x1, local copies, waits for them, and re-layouts: 18.4 us -> 1.71 us  [local(): lax.all_to_all(jnp.stack(jnp.split(frequency_filter(local_spectrum, band_...]
    convert_element_type x3 -> x0, local copies, waits for them, and re-layouts: 15 us -> none  [the longest x1 11.3 us: frequency_filter(): return restored.astype(jnp.bfloat16)]
    unnamed x15 -> x26, local copies, waits for them, and re-layouts: 21.9 us -> 14.7 us
where the time goes in v1:
time: 800 us; the launch traced here: 791 us
  other arithmetic  252 us (32%)
  matrix products  218 us (27%)
  waiting for transfers between devices  151 us (19%)
  blocking collectives  67.2 us (8%)
  local copies, waits for them, and re-layouts  63.6 us (8%)
  starting transfers between devices  18.4 us (2%)
  between operations  14.9 us (2%)
    another operation x13, other arithmetic  211 us
    psum x1, waiting for transfers between devices, local(): lax.psum((spectra, gram_matrix, trace_power), 'chan')  82 us
    psum x1, blocking collectives, local(): lax.psum((spectra, gram_matrix, trace_power), 'chan')  67.2 us
    all_to_all x1, waiting for transfers between devices, local(): lax.all_to_all(spectrum, 'chan', split_axis=1, concat_axis=2, tiled=True)  38 us
    dot_general x4, matrix products, project(): jnp.einsum('kml,rfl->krfm', members, dft_table, preferred_element_type=jn...  36.2 us
    dot_general x4, matrix products, temporal_advance(): jnp.einsum(layout, dft_table, segment, preferred_element_type=jnp.float32)  32.2 us
    all_to_all x1, waiting for transfers between devices, local(): lax.all_to_all(jnp.stack(jnp.split(frequency_filter(local_spectrum, band_...  30.6 us
    dot_general x4, matrix products, rotate(): sin_imag = jnp.einsum(layout, sin_table, imag_part, precision=highest)  30.2 us
  transfers between devices with their start and end apart: 3, of which 3 were waited for; matrix products, arithmetic and copies ran while one was open for 2% of the time, Pallas kernels for 0%

profile of v1, /device:TPU:0, one launch (start us, length us, event | category | flops | bytes accessed | tf_op | source)
XLA Modules:
  0.0 790.8 jit_solution(15219746097190486472)
XLA Ops:
  7.2 148.7 %while.40 = (s32[]{:T(128)}, f32[2,768,640]{2,1,0:T(8,128)}, s32[4]{0:T(128)S(1)}, bf16[640,7680]{1,0:T(8,128)(2,1)}, s32[]{:T(128)}, /*index=5*/s32[]{:T(128)}, s32[1]{0:T(128)}, s32[]{:T(128)}) while((s32[]{:T(128)}, f32[2,768,640]{2,1,0:T(8,128)}, s32[4]{0:T(128)S(1)}, bf16[640,7680]{1,0:T(8,128)(2,1)}, s32[]{:T(128)}, ...), condition=%wide.region_1.2_spmd.clone.clone, body=%wide.region_0.1_spmd.clone.clone.sunk | while | flops 3806337792 | bytes 53588192 | solution.py:60
  8.5 25.9 %fusion.349 = (bf16[1,768,1920]{2,1,0:T(8,128)(2,1)S(1)}, bf16[1,768,1920]{2,1,0:T(8,128)(2,1)S(1)}) fusion(f32[768]{0:T(1024)S(1)} %get-tuple-element.485, f32[768]{0:T(1024)S(1)} %get-tuple-element.486), kind=kLoop, calls=%fused_computation.52.clone.1 | loop fusion | flops 26542080 | bytes 5904384 | tf_op jit(solution)/shard_map/convert
  34.5 8.1 %select_add_fusion.2 = f32[2,768,640]{2,1,0:T(8,128)S(1)} fusion(f32[2,768,640]{2,1,0:T(8,128)S(1)} %copy-done.4, pred[]{:T(512)S(6)} %compare.24, bf16[640,7680]{1,0:T(8,128)(2,1)} %get-tuple-element.508, s32[]{:T(128)S(6)} %select_n.428, bf16[1,768,1920]{2,1,0:T(8,128)(2,1)S(1)} %get-tuple-element.487, ...), kind=kOutput, calls=%fused_computation.64.clone.1 | convolution fusion | flops 3779788800 | bytes 16220165 | tf_op jit(solution)/shard_map/while/body/eval_jaxpr/rft,mt->rfm/dot_general | solution.py:56
  42.5 1.9 copy-done.5
  45.7 25.9 %fusion.349 = (bf16[1,768,1920]{2,1,0:T(8,128)(2,1)S(1)}, bf16[1,768,1920]{2,1,0:T(8,128)(2,1)S(1)}) fusion(f32[768]{0:T(1024)S(1)} %get-tuple-element.485, f32[768]{0:T(1024)S(1)} %get-tuple-element.486), kind=kLoop, calls=%fused_computation.52.clone.1 | loop fusion | flops 26542080 | bytes 5904384 | tf_op jit(solution)/shard_map/convert
  71.6 8.0 %select_add_fusion.2 = f32[2,768,640]{2,1,0:T(8,128)S(1)} fusion(f32[2,768,640]{2,1,0:T(8,128)S(1)} %copy-done.4, pred[]{:T(512)S(6)} %compare.24, bf16[640,7680]{1,0:T(8,128)(2,1)} %get-tuple-element.508, s32[]{:T(128)S(6)} %select_n.428, bf16[1,768,1920]{2,1,0:T(8,128)(2,1)S(1)} %get-tuple-element.487, ...), kind=kOutput, calls=%fused_computation.64.clone.1 | convolution fusion | flops 3779788800 | bytes 16220165 | tf_op jit(solution)/shard_map/while/body/eval_jaxpr/rft,mt->rfm/dot_general | solution.py:56
  82.9 25.9 %fusion.349 = (bf16[1,768,1920]{2,1,0:T(8,128)(2,1)S(1)}, bf16[1,768,1920]{2,1,0:T(8,128)(2,1)S(1)}) fusion(f32[768]{0:T(1024)S(1)} %get-tuple-element.485, f32[768]{0:T(1024)S(1)} %get-tuple-element.486), kind=kLoop, calls=%fused_computation.52.clone.1 | loop fusion | flops 26542080 | bytes 5904384 | tf_op jit(solution)/shard_map/convert
  108.8 8.1 %select_add_fusion.2 = f32[2,768,640]{2,1,0:T(8,128)S(1)} fusion(f32[2,768,640]{2,1,0:T(8,128)S(1)} %copy-done.4, pred[]{:T(512)S(6)} %compare.24, bf16[640,7680]{1,0:T(8,128)(2,1)} %get-tuple-element.508, s32[]{:T(128)S(6)} %select_n.428, bf16[1,768,1920]{2,1,0:T(8,128)(2,1)S(1)} %get-tuple-element.487, ...), kind=kOutput, calls=%fused_computation.64.clone.1 | convolution fusion | flops 3779788800 | bytes 16220165 | tf_op jit(solution)/shard_map/while/body/eval_jaxpr/rft,mt->rfm/dot_general | solution.py:56
  120.1 25.9 %fusion.349 = (bf16[1,768,1920]{2,1,0:T(8,128)(2,1)S(1)}, bf16[1,768,1920]{2,1,0:T(8,128)(2,1)S(1)}) fusion(f32[768]{0:T(1024)S(1)} %get-tuple-element.485, f32[768]{0:T(1024)S(1)} %get-tuple-element.486), kind=kLoop, calls=%fused_computation.52.clone.1 | loop fusion | flops 26542080 | bytes 5904384 | tf_op jit(solution)/shard_map/convert
  146.0 8.0 %select_add_fusion.2 = f32[2,768,640]{2,1,0:T(8,128)S(1)} fusion(f32[2,768,640]{2,1,0:T(8,128)S(1)} %copy-done.4, pred[]{:T(512)S(6)} %compare.24, bf16[640,7680]{1,0:T(8,128)(2,1)} %get-tuple-element.508, s32[]{:T(128)S(6)} %select_n.428, bf16[1,768,1920]{2,1,0:T(8,128)(2,1)S(1)} %get-tuple-element.487, ...), kind=kOutput, calls=%fused_computation.64.clone.1 | convolution fusion | flops 3779788800 | bytes 16220165 | tf_op jit(solution)/shard_map/while/body/eval_jaxpr/rft,mt->rfm/dot_general | solution.py:56
  154.1 1.9 copy-done.5
  155.9 6.4 copy.113
  162.4 7.6 all-to-all-start
  170.5 38.0 %all-to-all-done = bf16[2,768,640]{2,0,1:T(2,128)(2,1)S(1)} async-done(((bf16[2,768,640]{2,0,1:T(2,128)(2,1)}), bf16[2,768,640]{2,0,1:T(2,128)(2,1)S(1)}, u32[]{:S(2)}, u32[]{:S(2)}) %all-to-all-start) | async-done | bytes 1966112 | tf_op jit(solution)/shard_map/all_to_all | solution.py:158
  213.6 11.9 %fusion.89 = f32[48,16,640]{2,1,0:T(8,128)S(1)} fusion(f32[48,640,16]{1,2,0:T(8,128)S(1)} %multiply_add_fusion.1, f32[48,640,16]{1,2,0:T(8,128)S(1)} %multiply_subtract_fusion.1, f32[16,640]{1,0:T(8,128)S(1)} %get-tuple-element.371, f32[16,640]{1,0:T(8,128)S(1)} %get-tuple-element.370), kind=kOutput, calls=%fused_computation.124 | convolution fusion | flops 3780034560 | bytes 5980160 | tf_op jit(solution)/shard_map/mn,fkm->fkn/dot_general | solution.py:22
  225.5 11.7 %fusion.91 = f32[48,16,640]{2,1,0:T(8,128)S(1)} fusion(f32[48,640,16]{1,2,0:T(8,128)S(1)} %multiply_add_fusion.1, f32[48,640,16]{1,2,0:T(8,128)S(1)} %multiply_subtract_fusion.1, f32[16,640]{1,0:T(8,128)S(1)} %get-tuple-element.371, f32[16,640]{1,0:T(8,128)S(1)} %get-tuple-element.370), kind=kOutput, calls=%fused_computation.126 | convolution fusion | flops 3780034560 | bytes 5980160 | tf_op jit(solution)/shard_map/mn,fkm->fkn/dot_general | solution.py:23
  237.3 11.8 %add_select_fusion.6 = f32[48,16,640]{2,1,0:T(8,128)S(1)} fusion(f32[48,16,640]{2,1,0:T(8,128)S(1)} %fusion.89, s32[16,640]{1,0:T(8,128)S(1)} %compare_select_fusion, s32[48]{0:T(128)S(1)} %get-tuple-element.367, s32[48]{0:T(128)S(1)} %get-tuple-element.366, f32[48,640,16]{1,2,0:T(8,128)S(1)} %multiply_add_fusion.1, ...), kind=kOutput, calls=%fused_computation.113 | convolution fusion | flops 3782983680 | bytes 7987584 | tf_op jit(solution)/shard_map/mn,fkm->fkn/dot_general | solution.py:21
  249.0 11.8 %fusion.87 = f32[48,16,640]{2,1,0:T(8,128)S(1)} fusion(f32[48,16,640]{2,1,0:T(8,128)S(1)} %add_select_fusion.6), kind=kOutput, calls=%fused_computation.122 | convolution fusion | flops 3778560000 | bytes 3932160 | tf_op jit(solution)/shard_map/mn,fkn->fkm/dot_general | solution.py:23
  260.9 11.7 %subtract_select_fusion = f32[48,16,640]{2,1,0:T(8,128)S(1)} fusion(f32[48,16,640]{2,1,0:T(8,128)S(1)} %fusion.91, s32[16,640]{1,0:T(8,128)S(1)} %compare_select_fusion, s32[48]{0:T(128)S(1)} %get-tuple-element.367, s32[48]{0:T(128)S(1)} %get-tuple-element.366, f32[48,640,16]{1,2,0:T(8,128)S(1)} %multiply_add_fusion.1, ...), kind=kOutput, calls=%fused_computation.114 | convolution fusion | flops 3782983680 | bytes 7987584 | tf_op jit(solution)/shard_map/mn,fkm->fkn/dot_general | solution.py:20
  272.6 11.6 %fusion.85 = f32[48,16,640]{2,1,0:T(8,128)S(1)} fusion(f32[48,16,640]{2,1,0:T(8,128)S(1)} %subtract_select_fusion), kind=kOutput, calls=%fused_computation.120 | convolution fusion | flops 3778560000 | bytes 3932160 | tf_op jit(solution)/shard_map/mn,fkn->fkm/dot_general | solution.py:22
  284.2 11.9 %fusion.114 = f32[48,16,640]{2,1,0:T(8,128)S(1)} fusion(f32[48,16,640]{2,1,0:T(8,128)S(1)} %fusion.87, f32[48,16,640]{2,1,0:T(8,128)S(1)} %subtract_select_fusion), kind=kOutput, calls=%fused_computation.142 | convolution fusion | flops 3779051520 | bytes 5898240 | tf_op jit(solution)/shard_map/mn,fkn->fkm/dot_general | solution.py:20
  296.2 11.5 %fusion.117 = f32[48,16,640]{2,1,0:T(8,128)S(1)} fusion(f32[48,16,640]{2,1,0:T(8,128)S(1)} %fusion.85, f32[48,16,640]{2,1,0:T(8,128)S(1)} %add_select_fusion.6), kind=kOutput, calls=%fused_computation.143 | convolution fusion | flops 3779051520 | bytes 5898240 | tf_op jit(solution)/shard_map/mn,fkn->fkm/dot_general | solution.py:21
  307.7 2.0 fusion.185
  309.8 3.3 fusion.184
  313.1 3.3 add_bitcast_fusion.1
  316.4 2.8 stack.95
  319.2 5.5 subtract_bitcast_fusion.1
  324.7 2.9 stack.94
  327.6 2.1 fusion.80
  340.3 10.7 %all-to-all-start.1 = ((bf16[16,2,48,640]{3,2,1,0:T(8,128)(2,1)}), bf16[16,2,48,640]{3,2,1,0:T(8,128)(2,1)}, u32[]{:S(2)}, u32[]{:S(2)}) async-start(bf16[16,2,48,640]{3,2,1,0:T(8,128)(2,1)} %fusion.190), calls=%async_computation.1 | async-start | bytes 3932160 | tf_op jit(solution)/shard_map/all_to_all | solution.py:162
  351.1 2.8 negate_convert_fusion
  354.1 5.1 fusion.142
  359.2 30.6 %all-to-all-done.1 = bf16[16,2,48,640]{3,2,1,0:T(8,128)(2,1)} async-done(((bf16[16,2,48,640]{3,2,1,0:T(8,128)(2,1)}), bf16[16,2,48,640]{3,2,1,0:T(8,128)(2,1)}, u32[]{:S(2)}, u32[]{:S(2)}) %all-to-all-start.1) | async-done | bytes 1966112 | tf_op jit(solution)/shard_map/all_to_all | solution.py:162
  393.2 4.1 copy.54
  397.3 126.7 %while.39 = (s32[]{:T(128)}, f32[4,1920]{1,0:T(4,128)S(1)}, s32[4]{0:T(128)S(1)}, bf16[2,768,640]{1,2,0:T(8,128)(2,1)}, s32[]{:T(128)}, /*index=5*/s32[1]{0:T(128)}, s32[]{:T(128)}) while((s32[]{:T(128)}, f32[4,1920]{1,0:T(4,128)S(1)}, s32[4]{0:T(128)S(1)}, bf16[2,768,640]{1,2,0:T(8,128)(2,1)}, s32[]{:T(128)}, ...), condition=%wide.region_11.12_spmd.clone.clone, body=%wide.region_9.11_spmd.clone.clone.sunk | while | flops 3808056064 | bytes 21677712 | solution.py:141
  398.6 25.9 %fusion.344 = (bf16[1,768,1920]{2,1,0:T(8,128)(2,1)S(1)}, bf16[1,768,1920]{2,1,0:T(8,128)(2,1)S(1)}) fusion(f32[768]{0:T(1024)S(1)} %get-tuple-element.477, f32[768]{0:T(1024)S(1)} %get-tuple-element.478), kind=kLoop, calls=%fused_computation.16.clone.1 | loop fusion | flops 26542080 | bytes 5904384 | tf_op jit(solution)/shard_map/convert.2
  424.6 4.3 fusion.345
  430.3 25.9 %fusion.344 = (bf16[1,768,1920]{2,1,0:T(8,128)(2,1)S(1)}, bf16[1,768,1920]{2,1,0:T(8,128)(2,1)S(1)}) fusion(f32[768]{0:T(1024)S(1)} %get-tuple-element.477, f32[768]{0:T(1024)S(1)} %get-tuple-element.478), kind=kLoop, calls=%fused_computation.16.clone.1 | loop fusion | flops 26542080 | bytes 5904384 | tf_op jit(solution)/shard_map/convert.2
  456.2 4.3 fusion.345
  462.0 25.9 %fusion.344 = (bf16[1,768,1920]{2,1,0:T(8,128)(2,1)S(1)}, bf16[1,768,1920]{2,1,0:T(8,128)(2,1)S(1)}) fusion(f32[768]{0:T(1024)S(1)} %get-tuple-element.477, f32[768]{0:T(1024)S(1)} %get-tuple-element.478), kind=kLoop, calls=%fused_computation.16.clone.1 | loop fusion | flops 26542080 | bytes 5904384 | tf_op jit(solution)/shard_map/convert.2
  487.9 4.3 fusion.345
  493.6 25.9 %fusion.344 = (bf16[1,768,1920]{2,1,0:T(8,128)(2,1)S(1)}, bf16[1,768,1920]{2,1,0:T(8,128)(2,1)S(1)}) fusion(f32[768]{0:T(1024)S(1)} %get-tuple-element.477, f32[768]{0:T(1024)S(1)} %get-tuple-element.478), kind=kLoop, calls=%fused_computation.16.clone.1 | loop fusion | flops 26542080 | bytes 5904384 | tf_op jit(solution)/shard_map/convert.2
  519.6 4.3 fusion.345
  524.0 67.2 %all-reduce.1 = (f32[16,16]{0,1:T(8,128)S(1)}, f32[7680]{0:T(1024)S(1)}) all-reduce(f32[16,16]{0,1:T(8,128)S(1)} %fusion.142, f32[7680]{0:T(1024)S(1)} %reshape.553), channel_id=1, replica_groups=mesh['groups'=2,'chan'=16] {'chan'}, use_global_device_ids=true, to_apply=%region_5.6 | all-reduce | flops 7936 | bytes 63488 | tf_op jit(solution)/shard_map/psum | solution.py:178
  595.1 84.8 %while.38 = (s32[]{:T(128)}, f32[4,4,2,768]{3,2,1,0:T(2,128)S(1)}, bf16[4,4,640,200]{2,3,1,0:T(8,128)(2,1)}, bf16[2,768,200]{1,2,0:T(8,128)(2,1)S(1)}, f32[768,640]{1,0:T(8,128)}, /*index=5*/f32[768,640]{1,0:T(8,128)}, s32[]{:T(128)}) while((s32[]{:T(128)}, f32[4,4,2,768]{3,2,1,0:T(2,128)S(1)}, bf16[4,4,640,200]{2,3,1,0:T(8,128)(2,1)}, ...), condition=%wide.region_3.4_spmd, body=%wide.region_2.3_spmd.sunk | while | flops 1588592640 | bytes 45113436 | solution.py:123
  595.1 9.1 %convolution_bitcast_fusion.2 = f32[4,2,768,640]{2,3,1,0:T(8,128)} fusion(bf16[4,4,640,200]{2,3,1,0:T(8,128)(2,1)} %get-tuple-element.550, s32[]{:T(128)S(6)} %copy.154, bf16[2,768,200]{1,2,0:T(8,128)(2,1)S(1)} %get-tuple-element.551), kind=kOutput, calls=%fused_computation.79.clone.1 | convolution fusion | flops 1572864000 | bytes 17367044 | tf_op jit(solution)/shard_map/while/body/eval_jaxpr/kml,rfl->krfm/dot_general | solution.py:111
  604.1 1.9 copy.121
  606.0 2.9 copy.122
  609.0 7.2 multiply_reduce_fusion.5
  616.3 9.1 %convolution_bitcast_fusion.2 = f32[4,2,768,640]{2,3,1,0:T(8,128)} fusion(bf16[4,4,640,200]{2,3,1,0:T(8,128)(2,1)} %get-tuple-element.550, s32[]{:T(128)S(6)} %copy.154, bf16[2,768,200]{1,2,0:T(8,128)(2,1)S(1)} %get-tuple-element.551), kind=kOutput, calls=%fused_computation.79.clone.1 | convolution fusion | flops 1572864000 | bytes 17367044 | tf_op jit(solution)/shard_map/while/body/eval_jaxpr/kml,rfl->krfm/dot_general | solution.py:111
  625.3 1.9 copy.121
  627.2 2.9 copy.122
  630.2 7.2 multiply_reduce_fusion.5
  637.5 9.1 %convolution_bitcast_fusion.2 = f32[4,2,768,640]{2,3,1,0:T(8,128)} fusion(bf16[4,4,640,200]{2,3,1,0:T(8,128)(2,1)} %get-tuple-element.550, s32[]{:T(128)S(6)} %copy.154, bf16[2,768,200]{1,2,0:T(8,128)(2,1)S(1)} %get-tuple-element.551), kind=kOutput, calls=%fused_computation.79.clone.1 | convolution fusion | flops 1572864000 | bytes 17367044 | tf_op jit(solution)/shard_map/while/body/eval_jaxpr/kml,rfl->krfm/dot_general | solution.py:111
  646.5 1.9 copy.121
  648.4 2.9 copy.122
  651.3 7.2 multiply_reduce_fusion.5
  658.7 9.1 %convolution_bitcast_fusion.2 = f32[4,2,768,640]{2,3,1,0:T(8,128)} fusion(bf16[4,4,640,200]{2,3,1,0:T(8,128)(2,1)} %get-tuple-element.550, s32[]{:T(128)S(6)} %copy.154, bf16[2,768,200]{1,2,0:T(8,128)(2,1)S(1)} %get-tuple-element.551), kind=kOutput, calls=%fused_computation.79.clone.1 | convolution fusion | flops 1572864000 | bytes 17367044 | tf_op jit(solution)/shard_map/while/body/eval_jaxpr/kml,rfl->krfm/dot_general | solution.py:111
  667.7 1.9 copy.121
  669.6 2.9 copy.122
  672.5 7.2 multiply_reduce_fusion.5
  684.7 82.0 %all-reduce.4.cloned.1.call-done = f32[16,2,768]{2,1,0:T(2,128)} async-done(((f32[16,2,768]{2,1,0:T(2,128)}), f32[16,2,768]{2,1,0:T(2,128)}) %all-reduce.4.cloned.1.call-update) | async-done | bytes 98320 | tf_op jit(solution)/shard_map/psum | solution.py:178
  767.8 6.9 fusion.122
  774.7 7.7 broadcast_divide_fusion
  (135 shorter events, 40.3 us)
Async XLA Ops:
  7.2 162.8 %copy-start = (s32[2,768]{1,0:T(2,128)S(1)}, s32[2,768]{1,0:T(2,128)}, u32[]{:S(2)}) copy-start(s32[2,768]{1,0:T(2,128)} %param.11) | copy-start | bytes 18436
  8.5 25.9 %copy-start.4 = (f32[2,768,640]{2,1,0:T(8,128)S(1)}, f32[2,768,640]{2,1,0:T(8,128)}, u32[]{:S(2)}) copy-start(f32[2,768,640]{2,1,0:T(8,128)} %get-tuple-element.498) | copy-start | bytes 11796484 | tf_op jit(solution)/shard_map/while
  42.5 1.9 copy-start.5
  45.7 25.9 %copy-start.4 = (f32[2,768,640]{2,1,0:T(8,128)S(1)}, f32[2,768,640]{2,1,0:T(8,128)}, u32[]{:S(2)}) copy-start(f32[2,768,640]{2,1,0:T(8,128)} %get-tuple-element.498) | copy-start | bytes 11796484 | tf_op jit(solution)/shard_map/while
  79.7 1.9 copy-start.5
  82.9 25.9 %copy-start.4 = (f32[2,768,640]{2,1,0:T(8,128)S(1)}, f32[2,768,640]{2,1,0:T(8,128)}, u32[]{:S(2)}) copy-start(f32[2,768,640]{2,1,0:T(8,128)} %get-tuple-element.498) | copy-start | bytes 11796484 | tf_op jit(solution)/shard_map/while
  116.9 1.9 copy-start.5
  120.1 25.9 %copy-start.4 = (f32[2,768,640]{2,1,0:T(8,128)S(1)}, f32[2,768,640]{2,1,0:T(8,128)}, u32[]{:S(2)}) copy-start(f32[2,768,640]{2,1,0:T(8,128)} %get-tuple-element.498) | copy-start | bytes 11796484 | tf_op jit(solution)/shard_map/while
  154.1 1.9 copy-start.5
  162.4 46.1 %all-to-all-start = ((bf16[2,768,640]{2,0,1:T(2,128)(2,1)}), bf16[2,768,640]{2,0,1:T(2,128)(2,1)S(1)}, u32[]{:S(2)}, u32[]{:S(2)}) async-start(bf16[2,768,640]{2,0,1:T(2,128)(2,1)} %copy.113), calls=%async_computation | async-start | bytes 3932160 | tf_op jit(solution)/shard_map/all_to_all | solution.py:158
  307.7 5.4 copy-start.2
  324.7 2.9 copy-start.3
  340.3 49.5 %all-to-all-start.1 = ((bf16[16,2,48,640]{3,2,1,0:T(8,128)(2,1)}), bf16[16,2,48,640]{3,2,1,0:T(8,128)(2,1)}, u32[]{:S(2)}, u32[]{:S(2)}) async-start(bf16[16,2,48,640]{3,2,1,0:T(8,128)(2,1)} %fusion.190), calls=%async_computation.1 | async-start | bytes 3932160 | tf_op jit(solution)/shard_map/all_to_all | solution.py:162
  351.0 415.7 %all-reduce.4.cloned.1.call-start = ((), (), s32[]{:S(2)}) async-start(), calls=%async_computation.2 | async-start | bytes 196608 | tf_op jit(solution)/shard_map/psum | solution.py:178
  398.6 25.9 %copy-start.6 = (bf16[2,768,640]{1,2,0:T(8,128)(2,1)S(1)}, bf16[2,768,640]{1,2,0:T(8,128)(2,1)}, u32[]{:S(2)}) copy-start(bf16[2,768,640]{1,2,0:T(8,128)(2,1)} %get-tuple-element.530) | copy-start | bytes 5898244 | tf_op jit(solution)/shard_map/while
  430.3 25.9 %copy-start.6 = (bf16[2,768,640]{1,2,0:T(8,128)(2,1)S(1)}, bf16[2,768,640]{1,2,0:T(8,128)(2,1)}, u32[]{:S(2)}) copy-start(bf16[2,768,640]{1,2,0:T(8,128)(2,1)} %get-tuple-element.530) | copy-start | bytes 5898244 | tf_op jit(solution)/shard_map/while
  462.0 25.9 %copy-start.6 = (bf16[2,768,640]{1,2,0:T(8,128)(2,1)S(1)}, bf16[2,768,640]{1,2,0:T(8,128)(2,1)}, u32[]{:S(2)}) copy-start(bf16[2,768,640]{1,2,0:T(8,128)(2,1)} %get-tuple-element.530) | copy-start | bytes 5898244 | tf_op jit(solution)/shard_map/while
  493.6 25.9 %copy-start.6 = (bf16[2,768,640]{1,2,0:T(8,128)(2,1)S(1)}, bf16[2,768,640]{1,2,0:T(8,128)(2,1)}, u32[]{:S(2)}) copy-start(bf16[2,768,640]{1,2,0:T(8,128)(2,1)} %get-tuple-element.530) | copy-start | bytes 5898244 | tf_op jit(solution)/shard_map/while
  679.9 0.6 copy-start.7
  774.7 8.7 %copy-start.1 = (s32[2,768]{1,0:T(2,128)S(1)}, s32[2,768]{1,0:T(2,128)}, u32[]{:S(2)}) copy-start(s32[2,768]{1,0:T(2,128)} %param.11) | copy-start | bytes 18436
Sparse Core Ops, SparseCore 0:
  680.6 86.0 all-reduce.3
